TPU v7x, 32 devices: a whole 2x2x4 slice. The times are simulated.
32 devices in a mesh: dp: 16 (over z, y, x), ctx: 2 (over core).
Axes of the slice: x: 2, y: 2, z: 4, core: 2. Of those that a mesh axis runs over, the one named last changes fastest.
Arguments:
- layer_in: bfloat16 [16, 256, 4096], P('dp', 'ctx'), may hold values from -6 to 6
- inner_act: bfloat16 [16, 256, 2176], P('dp', 'ctx'), may hold values from -6 to 6
- readout: bfloat16 [16, 256, 64], P('dp', 'ctx'), may hold values from -0.75 to 0.75
- w_in: bfloat16 [4096, 132], P('dp'), may hold values from -0.09375 to 0.09375
- a_log: float32 [68], replicated, may hold values from -3.9 to -1.6
- dt_bias: float32 [68], replicated, may hold values from -4 to -1
- d_skip: float32 [68], replicated, may hold values from 0.5 to 1.5
- grad_out: bfloat16 [16, 256, 2176], P('dp', 'ctx'), may hold values from -6 to 6
Outputs:
- grad_x: bfloat16 [16, 256, 2176], P('dp', 'ctx')
- grad_c: bfloat16 [16, 256, 64], P('dp', 'ctx')
- grad_proj: bfloat16 [16, 256, 132], P('dp', 'ctx')
- grad_w: float32 [4096, 132], P('dp', 'ctx')
All inputs are finite; a program needn't handle non-finite values.
Results may differ from a plain program's by a relative error of at most 0.015.
Values may be sent and summed in bfloat16 or wider, within the bound.
A program may use at most 64 MiB of HBM per device.

v0:
```python
import jax
import jax.numpy as jnp
from jax import lax
from jax.sharding import PartitionSpec as P

STATE = 64
BLOCK = 128


def entering(array, axis, join, neutral, backward):
    count = lax.axis_size(axis)
    place = lax.axis_index(axis)
    ahead = count - 1 - place if backward else place
    gathered = jax.tree.map(
        lambda a, kind: lax.all_gather(a.astype(kind), axis), array, (jnp.bfloat16, jnp.bfloat16)
    )
    state = jax.tree.map(lambda a, e: jnp.zeros_like(a) + jnp.asarray(e, a.dtype), array, neutral)

    def one(turn, state):
        source = count - 1 - turn if backward else turn
        return join(
            state,
            jax.tree.map(
                lambda a, own: lax.dynamic_index_in_dim(a, source, 0, False).astype(own.dtype),
                gathered,
                array,
            ),
        )

    return lax.fori_loop(0, ahead, one, state)


def prepare(projected, a_log, dt_bias):
    b_rows = projected[:, :STATE].astype(jnp.bfloat16)
    step_size = jax.nn.softplus(projected[:, STATE:] + dt_bias)
    decay_rate = -jnp.exp(a_log) * step_size
    return (b_rows, step_size, decay_rate)


def blocked(values, width):
    return values.reshape(values.shape[0] // BLOCK, BLOCK, width)


def split_blocks(projected, inner_rows, a_log, dt_bias):
    row_count = projected.shape[0]
    head_count = a_log.shape[0]
    head_width = inner_rows.shape[1] // head_count
    b_rows, step_size, decay_rate = prepare(projected, a_log, dt_bias)
    inner_blocks = inner_rows.reshape(row_count // BLOCK, BLOCK, head_count, head_width)
    step_blocks = jnp.swapaxes(blocked(step_size, head_count), 1, 2)
    cum_blocks = jnp.cumsum(jnp.swapaxes(blocked(decay_rate, head_count), 1, 2), axis=2)
    return (inner_blocks, blocked(b_rows, STATE), step_blocks, cum_blocks, decay_rate)


def state_input(inner_c, b_c, step_c, cum_c):
    to_end = jnp.exp(cum_c[:, -1:] - cum_c) * step_c
    weighted = (b_c.astype(jnp.float32)[None] * to_end[:, :, None]).astype(jnp.bfloat16)
    return jnp.einsum("shp,hsn->hpn", inner_c, weighted, preferred_element_type=jnp.float32)


def block_forward(projected, inner_rows, c_rows, a_log, dt_bias, d_skip, entry_state):
    row_count = projected.shape[0]
    inner_blocks, b_blocks, step_blocks, cum_blocks, decay_rate = split_blocks(
        projected, inner_rows, a_log, dt_bias
    )
    c_blocks = blocked(c_rows, STATE)
    position = jnp.arange(BLOCK)
    causal = position[:, None] >= position[None, :]

    def block_advance(carried, pieces):
        inner_c, b_c, c_c, step_c, cum_c = pieces
        scores = jnp.dot(c_c, b_c.T, preferred_element_type=jnp.float32)
        spread = cum_c[:, :, None] - cum_c[:, None, :]
        factor = jnp.where(causal, jnp.exp(jnp.where(causal, spread, 0.0)), 0.0)
        mixing = (scores[None] * factor * step_c[:, None, :]).astype(jnp.bfloat16)
        within = jnp.einsum("hts,shp->thp", mixing, inner_c, preferred_element_type=jnp.float32)
        added = state_input(inner_c, b_c, step_c, cum_c)
        carried_in = jnp.einsum(
            "tn,hpn->thp", c_c.astype(jnp.float32), carried, precision=lax.Precision.HIGHEST
        )
        carried_in = carried_in * jnp.exp(cum_c).T[:, :, None]
        result = (within + carried_in + d_skip[None, :, None] * inner_c.astype(jnp.float32)).astype(
            jnp.bfloat16
        )
        carried = jnp.exp(cum_c[:, -1])[:, None, None] * carried + added
        return (carried, result)

    final_state, outputs = lax.scan(
        block_advance, entry_state, (inner_blocks, b_blocks, c_blocks, step_blocks, cum_blocks)
    )
    return (outputs.reshape(row_count, inner_rows.shape[1]), final_state)


def local_summary(projected, inner_rows, a_log, dt_bias):
    inner_blocks, b_blocks, step_blocks, cum_blocks, decay_rate = split_blocks(
        projected, inner_rows, a_log, dt_bias
    )
    head_count = a_log.shape[0]
    head_width = inner_rows.shape[1] // head_count

    def local_advance(carried, pieces):
        inner_c, b_c, step_c, cum_c = pieces
        added = state_input(inner_c, b_c, step_c, cum_c)
        return (jnp.exp(cum_c[:, -1])[:, None, None] * carried + added, None)

    zero_state = jnp.zeros((head_count, head_width, STATE), jnp.float32)
    final_state, unused = lax.scan(
        local_advance, zero_state, (inner_blocks, b_blocks, step_blocks, cum_blocks)
    )
    return (jnp.exp(jnp.sum(decay_rate, axis=0)), final_state)


def entry_weights(projected, c_rows, grad_rows, a_log, dt_bias):
    b_rows, step_size, decay_rate = prepare(projected, a_log, dt_bias)
    row_count = projected.shape[0]
    head_count = a_log.shape[0]
    head_width = grad_rows.shape[1] // head_count
    growth = jnp.exp(jnp.cumsum(decay_rate, axis=0))
    weighted = (c_rows.astype(jnp.float32)[:, None, :] * growth[:, :, None]).astype(jnp.bfloat16)
    return jnp.einsum(
        "thp,thn->hpn",
        grad_rows.reshape(row_count, head_count, head_width),
        weighted,
        preferred_element_type=jnp.float32,
    )


def combine_carry(earlier, later):
    return (earlier[0] * later[0], later[1] + later[0][:, None, None] * earlier[1])


def pass_along(decay_total, summary, backward):
    identity = (jnp.ones_like(decay_total), jnp.zeros_like(summary))
    return entering((decay_total, summary), "ctx", combine_carry, identity, backward)


def per_device(layer_in, inner_act, readout, w_in, a_log, dt_bias, d_skip, grad_out):
    tokens = layer_in[0]
    inner_rows = inner_act[0]
    c_rows = readout[0]
    grad_rows = grad_out[0]
    w_full = lax.all_gather(w_in, "dp", axis=0, tiled=True)
    projected = jnp.dot(tokens, w_full, preferred_element_type=jnp.float32)
    decay_total, own_state = local_summary(projected, inner_rows, a_log, dt_bias)
    entry_part = entry_weights(projected, c_rows, grad_rows, a_log, dt_bias)
    entry_state = pass_along(decay_total, own_state, False)[1]
    exit_grad = pass_along(decay_total, entry_part, True)[1]

    def recompute(proj_val, inner_val, c_val):
        return block_forward(proj_val, inner_val, c_val, a_log, dt_bias, d_skip, entry_state)

    primal, pullback = jax.vjp(recompute, projected, inner_rows, c_rows)
    grad_p, grad_v, grad_r = pullback((grad_rows, exit_grad))
    proj_grad = grad_p.astype(jnp.bfloat16)
    seq_count = lax.axis_size("dp")
    contract = (((0,), (0,)), ((), ()))
    summed = lax.psum_scatter(
        lax.dot_general(tokens, proj_grad, contract, preferred_element_type=jnp.float32),
        "dp",
        scatter_dimension=0,
        tiled=True,
    )
    weight_grad = lax.psum_scatter(summed, "ctx", scatter_dimension=1, tiled=True)
    return (grad_v[None], grad_r[None], proj_grad[None], weight_grad / seq_count)


def solution(mesh):
    in_specs = (
        P("dp", "ctx", None),
        P("dp", "ctx", None),
        P("dp", "ctx", None),
        P("dp", None),
        P(),
        P(),
        P(),
        P("dp", "ctx", None),
    )
    out_specs = (P("dp", "ctx", None), P("dp", "ctx", None), P("dp", "ctx", None), P("dp", "ctx"))
    return jax.shard_map(
        per_device, mesh=mesh, in_specs=in_specs, out_specs=out_specs, check_vma=False
    )
```

profile of v0, /device:TPU:0, one launch (start us, length us, event | category | flops | bytes accessed | tf_op | source)
XLA Modules:
  0.0 213.8 jit_solution(7782846302152594224)
XLA Ops:
  8.0 1.4 copy.64
  12.5 56.9 %all-gather.5.cloned.1.call-done = bf16[4096,132]{0,1:T(8,128)(2,1)} async-done(((bf16[256,132]{0,1:T(8,128)(2,1)}), bf16[4096,132]{0,1:T(8,128)(2,1)}) %all-gather.5.cloned.1.call-update) | async-done | bytes 1081360 | tf_op jit(solution)/shard_map/all_gather | solution.py:142
  69.4 1.7 fusion.46
  74.6 2.6 %all-gather = bf16[136,32,64]{2,1,0:T(8,128)(2,1)S(1)} all-gather(bf16[68,32,64]{2,1,0:T(8,128)(2,1)S(1)} %fusion.29), channel_id=2, replica_groups=mesh['dp'=16,'ctx'=2] {'ctx'}, dimensions={0}, use_global_device_ids=true | all-gather | bytes 835584 | tf_op jit(solution)/shard_map/all_gather | solution.py:15
  77.5 2.4 %all-reduce.4 = bf16[136]{0:T(256)(128)(2,1)S(1)} all-reduce(bf16[136]{0:T(256)(128)(2,1)S(1)} %dynamic-update-slice), channel_id=3, replica_groups=mesh['dp'=16,'ctx'=2] {'ctx'}, use_global_device_ids=true, to_apply=%add.4 | all-reduce | flops 136 | bytes 544
  80.5 2.4 %fusion.13 = (f32[68,128]{1,0:T(8,128)}, bf16[128,64]{0,1:T(8,128)(2,1)}) fusion(f32[128,64]{0,1:T(8,128)} %fusion.68, f32[68,128]{1,0:T(8,128)} %copy.69, f32[68,32,64]{2,1,0:T(8,128)S(1)} %get-tuple-element.513, bf16[128,68,32]{0,2,1:T(8,128)(2,1)} %bitcast.174), kind=kOutput, calls=%fused_computation.23 | convolution fusion | flops 38419968 | bytes 1232896 | tf_op jit(solution)/shard_map/transpose(jvp())/while/body/eval_jaxpr/shp,hsn->hpn/dot_general | solution.py:58
  83.6 2.7 %all-gather.2 = bf16[136,32,64]{2,1,0:T(8,128)(2,1)} all-gather(bf16[68,32,64]{2,1,0:T(8,128)(2,1)S(1)} %fusion.28), channel_id=4, replica_groups=mesh['dp'=16,'ctx'=2] {'ctx'}, dimensions={0}, use_global_device_ids=true | all-gather | bytes 835584 | tf_op jit(solution)/shard_map/all_gather | solution.py:15
  92.7 1.5 copy.80
  94.2 1.6 copy.70
  95.7 6.0 %fusion.11 = (f32[68,128]{1,0:T(8,128)}, f32[68,128]{1,0:T(8,128)}, f32[68,128]{1,0:T(8,128)}, bf16[128,128]{1,0:T(8,128)(2,1)}) fusion(f32[68,128]{1,0:T(8,128)} %copy.73, f32[68,128]{1,0:T(8,128)} %bitcast.177, f32[128,128]{1,0:T(8,128)} %copy.70, pred[128,128]{1,0:T(8,128)(4,1)} %iota_compare_fusion, bf16[68,32,128]{2,1,0:T(8,128)(2,1)} %bitcast.164, ...), kind=kOutput, calls=%fused_computation.19 | convolution fusion | flops 90200576 | bytes 1402880 | tf_op jit(solution)/shard_map/transpose(jvp())/while/body/eval_jaxpr/hts,shp->thp/dot_general | solution.py:76
  101.7 1.5 copy.82
  103.2 1.5 copy.83
  104.7 1.6 fusion.57
  107.2 1.9 reduce_window_sum.37
  109.0 1.5 copy.85
  110.5 1.5 copy.79
  112.0 1.4 copy.86
  115.4 1.9 convolution_bitcast_fusion
  119.4 2.0 fusion.42
  121.4 1.5 fusion.44
  123.0 2.0 fusion.30
  125.5 72.9 %reduce-scatter.4.cloned.1.call-done = f32[256,132]{0,1:T(8,128)} async-done(((f32[4096,132]{0,1:T(8,128)}), f32[256,132]{0,1:T(8,128)}) %reduce-scatter.4.cloned.1.call-update) | async-done | bytes 135184 | tf_op jit(solution)/shard_map/reduce_scatter | solution.py:157
  198.4 3.6 %fusion = f32[256,72]{0,1:T(8,128)S(1)} fusion(f32[256,132]{0,1:T(8,128)} %reduce-scatter.4.cloned.1.call-done), kind=kCustom, calls=%all-reduce-scatter | all-reduce-scatter fusion | flops 36865 | bytes 209408
  202.0 2.3 %collective-permute-start = (f32[256,6]{0,1:T(8,128)S(1)}, f32[256,6]{0,1:T(8,128)S(1)}, u32[]{:S(2)}, u32[]{:S(2)}) collective-permute-start(f32[256,6]{0,1:T(8,128)S(1)} %slice.28), channel_id=1, source_target_pairs={{0,1},{2,3},{4,5},{6,7},{8,9},{10,11},{12,13},{14,15},{16,17},{18,... | collective-permute-start | bytes 18440
  (109 shorter events, 22.0 us)
Async XLA Ops:
  7.2 62.2 %copy-start = (bf16[1,128,4096]{2,1,0:T(8,128)(2,1)S(1)}, bf16[1,128,4096]{2,1,0:T(8,128)(2,1)}, u32[]{:S(2)}) copy-start(bf16[1,128,4096]{2,1,0:T(8,128)(2,1)} %param.12) | copy-start | bytes 3145732
  7.2 2.2 %copy-start.4 = (bf16[1,128,2176]{2,1,0:T(8,128)(2,1)S(1)}, bf16[1,128,2176]{2,1,0:T(8,128)(2,1)}, u32[]{:S(2)}) copy-start(bf16[1,128,2176]{2,1,0:T(8,128)(2,1)} %param.13) | copy-start | bytes 1671172
  7.2 62.2 %all-gather.5.cloned.1.call-start = ((), (), s32[]{:S(2)}) async-start(), calls=%async_computation.1 | async-start | bytes 1183744 | tf_op jit(solution)/shard_map/all_gather | solution.py:142
  7.9 190.4 %reduce-scatter.4.cloned.1.call-start = ((), (), s32[]{:S(2)}) async-start(), calls=%async_computation.2 | async-start | bytes 2367488 | tf_op jit(solution)/shard_map/reduce_scatter | solution.py:157
  8.0 2.5 %copy-start.24 = (u32[32]{0:T(128)S(1)}, u32[32]{0:T(128)}, u32[]{:S(2)}) copy-start(u32[32]{0:T(128)} %constant.223) | copy-start | bytes 388
  8.0 4.4 %copy-start.26 = (f32[68]{0:T(128)S(1)}, f32[68]{0:T(128)}, u32[]{:S(2)}) copy-start(f32[68]{0:T(128)} %param.16) | copy-start | bytes 820
  8.0 4.4 %copy-start.7 = (bf16[1,128,64]{1,2,0:T(8,128)(2,1)S(1)}, bf16[1,128,64]{1,2,0:T(8,128)(2,1)}, u32[]{:S(2)}) copy-start(bf16[1,128,64]{1,2,0:T(8,128)(2,1)} %param.14) | copy-start | bytes 49156
  9.4 64.6 %copy-start.1 = (bf16[1,128,2176]{1,2,0:T(8,128)(2,1)}, bf16[1,128,2176]{1,2,0:T(8,128)(2,1)S(1)}, u32[]{:S(2)}) copy-start(bf16[1,128,2176]{1,2,0:T(8,128)(2,1)S(1)} %copy.64) | copy-start | bytes 1671172
  12.4 59.4 %copy-start.23 = (f32[68]{0:T(128)}, f32[68]{0:T(128)S(1)}, u32[]{:S(2)}) copy-start(f32[68]{0:T(128)S(1)} %exponential_negate_fusion) | copy-start | bytes 820
  12.4 59.4 %copy-start.22 = (f32[68]{0:T(128)S(1)}, f32[68]{0:T(128)}, u32[]{:S(2)}) copy-start(f32[68]{0:T(128)} %param.17) | copy-start | bytes 820
  71.1 18.0 %copy-start.6 = (f32[128,132]{0,1:T(8,128)}, f32[128,132]{0,1:T(8,128)S(1)}, u32[]{:S(2)}) copy-start(f32[128,132]{0,1:T(8,128)S(1)} %fusion.46) | copy-start | bytes 202756
  72.9 18.6 %copy-start.21 = (f32[68]{0:T(128)}, f32[68]{0:T(128)S(1)}, u32[]{:S(2)}) copy-start(f32[68]{0:T(128)S(1)} %slice_bitcast_fusion) | copy-start | bytes 820
  80.5 2.4 %copy-start.5 = (bf16[1,128,2176]{1,2,0:T(8,128)(2,1)S(1)}, bf16[1,128,2176]{1,2,0:T(8,128)(2,1)}, u32[]{:S(2)}) copy-start(bf16[1,128,2176]{1,2,0:T(8,128)(2,1)} %copy.76) | copy-start | bytes 1671172
  80.5 2.4 %copy-start.13 = (f32[68,128]{1,0:T(8,128)S(1)}, f32[68,128]{1,0:T(8,128)}, u32[]{:S(2)}) copy-start(f32[68,128]{1,0:T(8,128)} %copy.69) | copy-start | bytes 104452
  80.5 2.4 %copy-start.15 = (f32[128,64]{0,1:T(8,128)S(1)}, f32[128,64]{0,1:T(8,128)}, u32[]{:S(2)}) copy-start(f32[128,64]{0,1:T(8,128)} %fusion.68) | copy-start | bytes 98308
  101.7 12.7 %copy-start.9 = (bf16[1,128,64]{1,2,0:T(8,128)(2,1)S(1)}, bf16[1,128,64]{1,2,0:T(8,128)(2,1)}, u32[]{:S(2)}) copy-start(bf16[1,128,64]{1,2,0:T(8,128)(2,1)} %param.14) | copy-start | bytes 49156
  119.4 2.0 copy-start.17
  119.4 3.6 %copy-start.3 = (bf16[1,128,2176]{1,2,0:T(8,128)(2,1)S(1)}, bf16[1,128,2176]{1,2,0:T(8,128)(2,1)}, u32[]{:S(2)}) copy-start(bf16[1,128,2176]{1,2,0:T(8,128)(2,1)} %copy-done.1) | copy-start | bytes 1671172
  119.4 3.5 %copy-start.12 = (f32[1,68,128]{2,1,0:T(8,128)S(1)}, f32[1,68,128]{2,1,0:T(8,128)}, u32[]{:S(2)}) copy-start(f32[1,68,128]{2,1,0:T(8,128)} %copy-done.11) | copy-start | bytes 104452
  119.4 3.5 %copy-start.18 = (f32[128,128]{1,0:T(8,128)S(1)}, f32[128,128]{1,0:T(8,128)}, u32[]{:S(2)}) copy-start(f32[128,128]{1,0:T(8,128)} %copy.70) | copy-start | bytes 196612
  119.4 3.5 %copy-start.19 = (f32[68,128]{1,0:T(8,128)S(1)}, f32[68,128]{1,0:T(8,128)}, u32[]{:S(2)}) copy-start(f32[68,128]{1,0:T(8,128)} %copy.73) | copy-start | bytes 104452
  119.4 3.5 %copy-start.20 = (pred[128,128]{1,0:T(8,128)(4,1)S(1)}, pred[128,128]{1,0:T(8,128)(4,1)}, u32[]{:S(2)}) copy-start(pred[128,128]{1,0:T(8,128)(4,1)} %iota_compare_fusion) | copy-start | bytes 49156
  123.0 2.0 copy-start.14
  202.0 4.1 %collective-permute-start = (f32[256,6]{0,1:T(8,128)S(1)}, f32[256,6]{0,1:T(8,128)S(1)}, u32[]{:S(2)}, u32[]{:S(2)}) collective-permute-start(f32[256,6]{0,1:T(8,128)S(1)} %slice.28), channel_id=1, source_target_pairs={{0,1},{2,3},{4,5},{6,7},{8,9},{10,11},{12,13},{14,15},{16,17},{18,... | collective-permute-start | bytes 18440
  (6 other events, 7.6 us)
Sparse Core Ops, SparseCore 0:
  10.7 58.5 all-gather.4
  117.5 80.8 reduce-scatter.3
where the time goes:
time: 215 us; the launch traced here: 214 us
  waiting for transfers between devices  130 us (60%)
  matrix products  22.4 us (10%)
  local copies, waits for them, and re-layouts  20.8 us (10%)
  between operations  15.9 us (7%)
  blocking collectives  11.4 us (5%)
  other arithmetic  10.2 us (5%)
  starting transfers between devices  2.33 us (1%)
    reduce_scatter x1, waiting for transfers between devices, per_device(): lax.psum_scatter(lax.dot_general(tokens, proj_grad, contract, preferred_e...  72.9 us
    all_gather x1, waiting for transfers between devices, per_device(): w_full = lax.all_gather(w_in, 'dp', axis=0, tiled=True)  56.9 us
    dot_general x2, matrix products, block_advance(): jnp.einsum('hts,shp->thp', mixing, inner_c, preferred_element_type=jnp.fl...  7.92 us
    unnamed x64, local copies, waits for them, and re-layouts  6.5 us
    unnamed x2, blocking collectives  6.08 us
    all_gather x2, blocking collectives, entering(): lax.all_gather(a.astype(kind), axis)  5.35 us
  transfers between devices with their start and end apart: 3, of which 2 were waited for; matrix products, arithmetic and copies ran while one was open for 6% of the time, Pallas kernels for 0%

commit v1 on v0

--- a/solution.py
+++ b/solution.py
@@ -5,6 +5,24 @@
 
 STATE = 64
 BLOCK = 128
+
+
+def gather_around(value, axis, dim):
+    ways, here, step = (lax.axis_size(axis), lax.axis_index(axis), value.shape[dim])
+    dims = [n * ways if d == dim else n for d, n in enumerate(value.shape)]
+    full = lax.dynamic_update_slice_in_dim(
+        jnp.zeros(dims, value.dtype), value, here * step, axis=dim
+    )
+    going_up = going_down = value
+    for far in range(1, ways // 2 + 1):
+        going_up = lax.ppermute(going_up, axis, [(d, (d + 1) % ways) for d in range(ways)])
+        full = lax.dynamic_update_slice_in_dim(full, going_up, (here - far) % ways * step, axis=dim)
+        if 2 * far < ways:
+            going_down = lax.ppermute(going_down, axis, [(d, (d - 1) % ways) for d in range(ways)])
+            full = lax.dynamic_update_slice_in_dim(
+                full, going_down, (here + far) % ways * step, axis=dim
+            )
+    return full
 
 
 def entering(array, axis, join, neutral, backward):
@@ -139,7 +157,7 @@
     inner_rows = inner_act[0]
     c_rows = readout[0]
     grad_rows = grad_out[0]
-    w_full = lax.all_gather(w_in, "dp", axis=0, tiled=True)
+    w_full = gather_around(w_in, "dp", 0)
     projected = jnp.dot(tokens, w_full, preferred_element_type=jnp.float32)
     decay_total, own_state = local_summary(projected, inner_rows, a_log, dt_bias)
     entry_part = entry_weights(projected, c_rows, grad_rows, a_log, dt_bias)

time: 215 us -> 223 us (1.037)
  starting transfers between devices: 2.33 us -> 43.3 us
  waiting for transfers between devices: 130 us -> 90.9 us
  other arithmetic: 10.2 us -> 14.2 us
  local copies, waits for them, and re-layouts: 20.8 us -> 23.9 us
    all_gather x1 -> x0, waiting for transfers between devices: 56.9 us -> none  [per_device(): w_full = lax.all_gather(w_in, 'dp', axis=0, tiled=True)]
    ppermute x0 -> x15, starting transfers between devices: none -> 41 us  [the longest x7 38 us: gather_around(): lax.ppermute(going_down, axis, [(d, (d - 1) % ways) for d in range(ways)])]
    ppermute x0 -> x15, waiting for transfers between devices: none -> 21.7 us  [the longest x8 21.7 us: gather_around(): lax.ppermute(going_up, axis, [(d, (d + 1) % ways) for d in range(ways)])]
    reduce_scatter x1, waiting for transfers between devices: 72.9 us -> 69.1 us  [per_device(): lax.psum_scatter(lax.dot_general(tokens, proj_grad, contract, preferred_e...]
    unnamed x64 -> x63, local copies, waits for them, and re-layouts: 6.5 us -> 7.28 us
  transfers between devices with their start and end apart: 3 -> 17, of which waited for: 2 -> 8; matrix products, arithmetic and copies ran while one was open for 6% -> 6% of each run, Pallas kernels for 0% -> 0%
where the time goes in v1:
time: 223 us; the launch traced here: 222 us
  waiting for transfers between devices  90.9 us (41%)
  starting transfers between devices  43.3 us (19%)
  local copies, waits for them, and re-layouts  23.9 us (11%)
  matrix products  21.4 us (10%)
  between operations  16 us (7%)
  other arithmetic  14.2 us (6%)
  blocking collectives  12.1 us (5%)
    reduce_scatter x1, waiting for transfers between devices, per_device(): lax.psum_scatter(lax.dot_general(tokens, proj_grad, contract, preferred_e...  69.1 us
    ppermute x7, starting transfers between devices, gather_around(): lax.ppermute(going_down, axis, [(d, (d - 1) % ways) for d in range(ways)])  38 us
    ppermute x8, waiting for transfers between devices, gather_around(): lax.ppermute(going_up, axis, [(d, (d + 1) % ways) for d in range(ways)])  21.7 us
    dot_general x2, matrix products, block_advance(): jnp.einsum('hts,shp->thp', mixing, inner_c, preferred_element_type=jnp.fl...  8.01 us
    unnamed x63, local copies, waits for them, and re-layouts  7.28 us
    unnamed x2, blocking collectives  6.08 us
    all_gather x2, blocking collectives, entering(): lax.all_gather(a.astype(kind), axis)  6.06 us
  transfers between devices with their start and end apart: 17, of which 8 were waited for; matrix products, arithmetic and copies ran while one was open for 6% of the time, Pallas kernels for 0%

profile of v1, /device:TPU:0, one launch (start us, length us, event | category | flops | bytes accessed | tf_op | source)
XLA Modules:
  0.0 222.1 jit_solution(11751471999530494873)
XLA Ops:
  7.2 3.0 %collective-permute-start = (bf16[256,132]{0,1:T(8,128)(2,1)}, bf16[256,132]{0,1:T(8,128)(2,1)S(1)}, u32[]{:S(2)}, u32[]{:S(2)}) collective-permute-start(bf16[256,132]{0,1:T(8,128)(2,1)} %param.15), channel_id=1, source_target_pairs={{0,2},{2,4},{4,6},{6,8},{8,10},{10,12},{12,14},{14,16},{16,18},{18... | collective-permute-start | bytes 202760 | tf_op jit(solution)/shard_map/ppermute | solution.py:18
  10.2 4.1 %collective-permute-start.1 = (bf16[256,132]{0,1:T(8,128)(2,1)}, bf16[256,132]{0,1:T(8,128)(2,1)S(1)}, u32[]{:S(2)}, u32[]{:S(2)}) collective-permute-start(bf16[256,132]{0,1:T(8,128)(2,1)} %param.15), channel_id=1, source_target_pairs={{0,30},{2,0},{4,2},{6,4},{8,6},{10,8},{12,10},{14,12},{16,14},{18,... | collective-permute-start | bytes 202760 | tf_op jit(solution)/shard_map/ppermute | solution.py:21
  20.2 5.6 %collective-permute-start.3 = (bf16[256,132]{0,1:T(8,128)(2,1)S(1)}, bf16[256,132]{0,1:T(8,128)(2,1)S(1)}, u32[]{:S(2)}, u32[]{:S(2)}) collective-permute-start(bf16[256,132]{0,1:T(8,128)(2,1)S(1)} %collective-permute-done.1), channel_id=1, source_target_pairs={{0,30},{2,0},{4,2},{6,4},{8,6},{10,8},{12,10},{14,12},{16,14},{18,... | collective-permute-start | bytes 202760 | tf_op jit(solution)/shard_map/ppermute | solution.py:21
  25.8 2.4 %collective-permute-done.2 = bf16[256,132]{0,1:T(8,128)(2,1)S(1)} collective-permute-done((bf16[256,132]{0,1:T(8,128)(2,1)S(1)}, bf16[256,132]{0,1:T(8,128)(2,1)S(1)}, u32[]{:S(2)}, u32[]{:S(2)}) %collective-permute-start.2) | collective-permute-done | bytes 67616 | tf_op jit(solution)/shard_map/ppermute | solution.py:18
  28.2 5.6 %collective-permute-start.5 = (bf16[256,132]{0,1:T(8,128)(2,1)S(1)}, bf16[256,132]{0,1:T(8,128)(2,1)S(1)}, u32[]{:S(2)}, u32[]{:S(2)}) collective-permute-start(bf16[256,132]{0,1:T(8,128)(2,1)S(1)} %collective-permute-done.3), channel_id=1, source_target_pairs={{0,30},{2,0},{4,2},{6,4},{8,6},{10,8},{12,10},{14,12},{16,14},{18,... | collective-permute-start | bytes 202760 | tf_op jit(solution)/shard_map/ppermute | solution.py:21
  33.8 2.2 %collective-permute-done.4 = bf16[256,132]{0,1:T(8,128)(2,1)S(1)} collective-permute-done((bf16[256,132]{0,1:T(8,128)(2,1)S(1)}, bf16[256,132]{0,1:T(8,128)(2,1)S(1)}, u32[]{:S(2)}, u32[]{:S(2)}) %collective-permute-start.4) | collective-permute-done | bytes 67616 | tf_op jit(solution)/shard_map/ppermute | solution.py:18
  36.1 5.6 %collective-permute-start.7 = (bf16[256,132]{0,1:T(8,128)(2,1)S(1)}, bf16[256,132]{0,1:T(8,128)(2,1)S(1)}, u32[]{:S(2)}, u32[]{:S(2)}) collective-permute-start(bf16[256,132]{0,1:T(8,128)(2,1)S(1)} %collective-permute-done.5), channel_id=1, source_target_pairs={{0,30},{2,0},{4,2},{6,4},{8,6},{10,8},{12,10},{14,12},{16,14},{18,... | collective-permute-start | bytes 202760 | tf_op jit(solution)/shard_map/ppermute | solution.py:21
  41.7 2.4 %collective-permute-done.6 = bf16[256,132]{0,1:T(8,128)(2,1)S(1)} collective-permute-done((bf16[256,132]{0,1:T(8,128)(2,1)S(1)}, bf16[256,132]{0,1:T(8,128)(2,1)S(1)}, u32[]{:S(2)}, u32[]{:S(2)}) %collective-permute-start.6) | collective-permute-done | bytes 67616 | tf_op jit(solution)/shard_map/ppermute | solution.py:18
  44.1 5.6 %collective-permute-start.9 = (bf16[256,132]{0,1:T(8,128)(2,1)S(1)}, bf16[256,132]{0,1:T(8,128)(2,1)S(1)}, u32[]{:S(2)}, u32[]{:S(2)}) collective-permute-start(bf16[256,132]{0,1:T(8,128)(2,1)S(1)} %collective-permute-done.7), channel_id=1, source_target_pairs={{0,30},{2,0},{4,2},{6,4},{8,6},{10,8},{12,10},{14,12},{16,14},{18,... | collective-permute-start | bytes 202760 | tf_op jit(solution)/shard_map/ppermute | solution.py:21
  49.7 2.2 %collective-permute-done.8 = bf16[256,132]{0,1:T(8,128)(2,1)S(1)} collective-permute-done((bf16[256,132]{0,1:T(8,128)(2,1)S(1)}, bf16[256,132]{0,1:T(8,128)(2,1)S(1)}, u32[]{:S(2)}, u32[]{:S(2)}) %collective-permute-start.8) | collective-permute-done | bytes 67616 | tf_op jit(solution)/shard_map/ppermute | solution.py:18
  52.0 5.7 %collective-permute-start.11 = (bf16[256,132]{0,1:T(8,128)(2,1)S(1)}, bf16[256,132]{0,1:T(8,128)(2,1)S(1)}, u32[]{:S(2)}, u32[]{:S(2)}) collective-permute-start(bf16[256,132]{0,1:T(8,128)(2,1)S(1)} %collective-permute-done.9), channel_id=1, source_target_pairs={{0,30},{2,0},{4,2},{6,4},{8,6},{10,8},{12,10},{14,12},{16,14},{18,... | collective-permute-start | bytes 202760 | tf_op jit(solution)/shard_map/ppermute | solution.py:21
  57.7 2.4 %collective-permute-done.10 = bf16[256,132]{0,1:T(8,128)(2,1)S(1)} collective-permute-done((bf16[256,132]{0,1:T(8,128)(2,1)S(1)}, bf16[256,132]{0,1:T(8,128)(2,1)S(1)}, u32[]{:S(2)}, u32[]{:S(2)}) %collective-permute-start.10) | collective-permute-done | bytes 67616 | tf_op jit(solution)/shard_map/ppermute | solution.py:18
  60.1 5.8 %collective-permute-start.13 = (bf16[256,132]{0,1:T(8,128)(2,1)S(1)}, bf16[256,132]{0,1:T(8,128)(2,1)S(1)}, u32[]{:S(2)}, u32[]{:S(2)}) collective-permute-start(bf16[256,132]{0,1:T(8,128)(2,1)S(1)} %collective-permute-done.11), channel_id=1, source_target_pairs={{0,30},{2,0},{4,2},{6,4},{8,6},{10,8},{12,10},{14,12},{16,14},{18,... | collective-permute-start | bytes 202760 | tf_op jit(solution)/shard_map/ppermute | solution.py:21
  65.9 2.2 %collective-permute-done.12 = bf16[256,132]{0,1:T(8,128)(2,1)S(1)} collective-permute-done((bf16[256,132]{0,1:T(8,128)(2,1)S(1)}, bf16[256,132]{0,1:T(8,128)(2,1)S(1)}, u32[]{:S(2)}, u32[]{:S(2)}) %collective-permute-start.12) | collective-permute-done | bytes 67616 | tf_op jit(solution)/shard_map/ppermute | solution.py:18
  68.2 7.9 %collective-permute-done.14 = bf16[256,132]{0,1:T(8,128)(2,1)S(1)} collective-permute-done((bf16[256,132]{0,1:T(8,128)(2,1)S(1)}, bf16[256,132]{0,1:T(8,128)(2,1)S(1)}, u32[]{:S(2)}, u32[]{:S(2)}) %collective-permute-start.14) | collective-permute-done | bytes 67616 | tf_op jit(solution)/shard_map/ppermute | solution.py:18
  80.2 2.6 %all-gather.2 = bf16[136,32,64]{2,1,0:T(8,128)(2,1)S(1)} all-gather(bf16[68,32,64]{2,1,0:T(8,128)(2,1)S(1)} %fusion.28), channel_id=4, replica_groups=mesh['dp'=16,'ctx'=2] {'ctx'}, dimensions={0}, use_global_device_ids=true | all-gather | bytes 835584 | tf_op jit(solution)/shard_map/all_gather | solution.py:33
  83.0 2.4 %all-reduce.4 = bf16[136]{0:T(256)(128)(2,1)S(1)} all-reduce(bf16[136]{0:T(256)(128)(2,1)S(1)} %dynamic-update-slice), channel_id=3, replica_groups=mesh['dp'=16,'ctx'=2] {'ctx'}, use_global_device_ids=true, to_apply=%add.4 | all-reduce | flops 136 | bytes 544
  88.3 3.5 %all-gather = bf16[136,32,64]{2,1,0:T(8,128)(2,1)} all-gather(bf16[68,32,64]{2,1,0:T(8,128)(2,1)S(1)} %fusion.29), channel_id=2, replica_groups=mesh['dp'=16,'ctx'=2] {'ctx'}, dimensions={0}, use_global_device_ids=true | all-gather | bytes 835584 | tf_op jit(solution)/shard_map/all_gather | solution.py:33
  93.5 2.3 %fusion.13 = (f32[68,128]{1,0:T(8,128)}, bf16[128,64]{0,1:T(8,128)(2,1)}) fusion(f32[128,64]{0,1:T(8,128)} %copy-done.14, f32[68,128]{1,0:T(8,128)S(1)} %copy-done.12, f32[68,32,64]{2,1,0:T(8,128)S(1)} %get-tuple-element.513, bf16[128,68,32]{0,2,1:T(8,128)(2,1)} %bitcast.179), kind=kOutput, calls=%fused_computation.23 | convolution fusion | flops 38419968 | bytes 1232896 | tf_op jit(solution)/shard_map/transpose(jvp())/while/body/eval_jaxpr/shp,hsn->hpn/dot_general | solution.py:76
  106.2 6.0 %fusion.11 = (f32[68,128]{1,0:T(8,128)}, f32[68,128]{1,0:T(8,128)}, f32[68,128]{1,0:T(8,128)}, bf16[128,128]{1,0:T(8,128)(2,1)}) fusion(f32[68,128]{1,0:T(8,128)} %copy.75, f32[68,128]{1,0:T(8,128)} %bitcast.181, f32[128,128]{1,0:T(8,128)} %copy.72, pred[128,128]{1,0:T(8,128)(4,1)} %iota_compare_fusion, bf16[68,32,128]{2,1,0:T(8,128)(2,1)} %bitcast.168, ...), kind=kOutput, calls=%fused_computation.19 | convolution fusion | flops 90200576 | bytes 1402880 | tf_op jit(solution)/shard_map/transpose(jvp())/while/body/eval_jaxpr/hts,shp->thp/dot_general | solution.py:94
  118.5 2.6 %reduce_window_sum.37 = f32[1,68,128]{2,1,0:T(8,128)} reduce-window(f32[1,68,128]{2,1,0:T(8,128)} %copy.86, f32[]{:T(128)} %constant.290.clone.1), window={size=1x1x128 pad=0_0x0_0x0_127}, to_apply=%region_15.16 | reduce-window | flops 1105408 | bytes 69636 | tf_op jit(solution)/shard_map/transpose(jvp(jit(cumsum)))/reduce_window_sum | solution.py:69
  137.5 69.1 %reduce-scatter.4.cloned.1.call-done = f32[256,132]{0,1:T(8,128)} async-done(((f32[4096,132]{0,1:T(8,128)}), f32[256,132]{0,1:T(8,128)}) %reduce-scatter.4.cloned.1.call-update) | async-done | bytes 135184 | tf_op jit(solution)/shard_map/reduce_scatter | solution.py:175
  206.7 3.6 %fusion = f32[256,72]{0,1:T(8,128)S(1)} fusion(f32[256,132]{0,1:T(8,128)} %reduce-scatter.4.cloned.1.call-done), kind=kCustom, calls=%all-reduce-scatter | all-reduce-scatter fusion | flops 36865 | bytes 209408
  210.3 2.3 %collective-permute-start.15 = (f32[256,6]{0,1:T(8,128)S(1)}, f32[256,6]{0,1:T(8,128)S(1)}, u32[]{:S(2)}, u32[]{:S(2)}) collective-permute-start(f32[256,6]{0,1:T(8,128)S(1)} %slice.28), channel_id=1, source_target_pairs={{0,1},{2,3},{4,5},{6,7},{8,9},{10,11},{12,13},{14,15},{16,17},{18,... | collective-permute-start | bytes 18440
  (152 shorter events, 50.2 us)
Async XLA Ops:
  7.2 68.9 %copy-start = (bf16[1,128,4096]{2,1,0:T(8,128)(2,1)S(1)}, bf16[1,128,4096]{2,1,0:T(8,128)(2,1)}, u32[]{:S(2)}) copy-start(bf16[1,128,4096]{2,1,0:T(8,128)(2,1)} %param.12) | copy-start | bytes 3145732
  7.2 9.2 %copy-start.5 = (bf16[1,128,2176]{2,1,0:T(8,128)(2,1)S(1)}, bf16[1,128,2176]{2,1,0:T(8,128)(2,1)}, u32[]{:S(2)}) copy-start(bf16[1,128,2176]{2,1,0:T(8,128)(2,1)} %param.19) | copy-start | bytes 1671172
  7.2 199.5 %reduce-scatter.4.cloned.1.call-start = ((), (), s32[]{:S(2)}) async-start(), calls=%async_computation.1 | async-start | bytes 2367488 | tf_op jit(solution)/shard_map/reduce_scatter | solution.py:175
  7.2 12.9 %collective-permute-start = (bf16[256,132]{0,1:T(8,128)(2,1)}, bf16[256,132]{0,1:T(8,128)(2,1)S(1)}, u32[]{:S(2)}, u32[]{:S(2)}) collective-permute-start(bf16[256,132]{0,1:T(8,128)(2,1)} %param.15), channel_id=1, source_target_pairs={{0,2},{2,4},{4,6},{6,8},{8,10},{10,12},{12,14},{14,16},{16,18},{18... | collective-permute-start | bytes 202760 | tf_op jit(solution)/shard_map/ppermute | solution.py:18
  10.2 9.9 %collective-permute-start.1 = (bf16[256,132]{0,1:T(8,128)(2,1)}, bf16[256,132]{0,1:T(8,128)(2,1)S(1)}, u32[]{:S(2)}, u32[]{:S(2)}) collective-permute-start(bf16[256,132]{0,1:T(8,128)(2,1)} %param.15), channel_id=1, source_target_pairs={{0,30},{2,0},{4,2},{6,4},{8,6},{10,8},{12,10},{14,12},{16,14},{18,... | collective-permute-start | bytes 202760 | tf_op jit(solution)/shard_map/ppermute | solution.py:21
  14.9 61.6 %copy-start.23 = (f32[68]{0:T(128)}, f32[68]{0:T(128)S(1)}, u32[]{:S(2)}) copy-start(f32[68]{0:T(128)S(1)} %exponential_negate_fusion) | copy-start | bytes 820
  16.3 62.6 %copy-start.6 = (bf16[1,128,2176]{1,2,0:T(8,128)(2,1)}, bf16[1,128,2176]{1,2,0:T(8,128)(2,1)S(1)}, u32[]{:S(2)}) copy-start(bf16[1,128,2176]{1,2,0:T(8,128)(2,1)S(1)} %copy.78) | copy-start | bytes 1671172
  20.1 8.0 %collective-permute-start.2 = (bf16[256,132]{0,1:T(8,128)(2,1)S(1)}, bf16[256,132]{0,1:T(8,128)(2,1)S(1)}, u32[]{:S(2)}, u32[]{:S(2)}) collective-permute-start(bf16[256,132]{0,1:T(8,128)(2,1)S(1)} %collective-permute-done), channel_id=1, source_target_pairs={{0,2},{2,4},{4,6},{6,8},{8,10},{10,12},{12,14},{14,16},{16,18},{18... | collective-permute-start | bytes 202760 | tf_op jit(solution)/shard_map/ppermute | solution.py:18
  20.2 8.0 %collective-permute-start.3 = (bf16[256,132]{0,1:T(8,128)(2,1)S(1)}, bf16[256,132]{0,1:T(8,128)(2,1)S(1)}, u32[]{:S(2)}, u32[]{:S(2)}) collective-permute-start(bf16[256,132]{0,1:T(8,128)(2,1)S(1)} %collective-permute-done.1), channel_id=1, source_target_pairs={{0,30},{2,0},{4,2},{6,4},{8,6},{10,8},{12,10},{14,12},{16,14},{18,... | collective-permute-start | bytes 202760 | tf_op jit(solution)/shard_map/ppermute | solution.py:21
  28.2 7.9 %collective-permute-start.4 = (bf16[256,132]{0,1:T(8,128)(2,1)S(1)}, bf16[256,132]{0,1:T(8,128)(2,1)S(1)}, u32[]{:S(2)}, u32[]{:S(2)}) collective-permute-start(bf16[256,132]{0,1:T(8,128)(2,1)S(1)} %collective-permute-done.2), channel_id=1, source_target_pairs={{0,2},{2,4},{4,6},{6,8},{8,10},{10,12},{12,14},{14,16},{16,18},{18... | collective-permute-start | bytes 202760 | tf_op jit(solution)/shard_map/ppermute | solution.py:18
  28.2 7.9 %collective-permute-start.5 = (bf16[256,132]{0,1:T(8,128)(2,1)S(1)}, bf16[256,132]{0,1:T(8,128)(2,1)S(1)}, u32[]{:S(2)}, u32[]{:S(2)}) collective-permute-start(bf16[256,132]{0,1:T(8,128)(2,1)S(1)} %collective-permute-done.3), channel_id=1, source_target_pairs={{0,30},{2,0},{4,2},{6,4},{8,6},{10,8},{12,10},{14,12},{16,14},{18,... | collective-permute-start | bytes 202760 | tf_op jit(solution)/shard_map/ppermute | solution.py:21
  36.1 8.0 %collective-permute-start.6 = (bf16[256,132]{0,1:T(8,128)(2,1)S(1)}, bf16[256,132]{0,1:T(8,128)(2,1)S(1)}, u32[]{:S(2)}, u32[]{:S(2)}) collective-permute-start(bf16[256,132]{0,1:T(8,128)(2,1)S(1)} %collective-permute-done.4), channel_id=1, source_target_pairs={{0,2},{2,4},{4,6},{6,8},{8,10},{10,12},{12,14},{14,16},{16,18},{18... | collective-permute-start | bytes 202760 | tf_op jit(solution)/shard_map/ppermute | solution.py:18
  36.1 8.0 %collective-permute-start.7 = (bf16[256,132]{0,1:T(8,128)(2,1)S(1)}, bf16[256,132]{0,1:T(8,128)(2,1)S(1)}, u32[]{:S(2)}, u32[]{:S(2)}) collective-permute-start(bf16[256,132]{0,1:T(8,128)(2,1)S(1)} %collective-permute-done.5), channel_id=1, source_target_pairs={{0,30},{2,0},{4,2},{6,4},{8,6},{10,8},{12,10},{14,12},{16,14},{18,... | collective-permute-start | bytes 202760 | tf_op jit(solution)/shard_map/ppermute | solution.py:21
  44.1 7.9 %collective-permute-start.8 = (bf16[256,132]{0,1:T(8,128)(2,1)S(1)}, bf16[256,132]{0,1:T(8,128)(2,1)S(1)}, u32[]{:S(2)}, u32[]{:S(2)}) collective-permute-start(bf16[256,132]{0,1:T(8,128)(2,1)S(1)} %collective-permute-done.6), channel_id=1, source_target_pairs={{0,2},{2,4},{4,6},{6,8},{8,10},{10,12},{12,14},{14,16},{16,18},{18... | collective-permute-start | bytes 202760 | tf_op jit(solution)/shard_map/ppermute | solution.py:18
  44.1 7.9 %collective-permute-start.9 = (bf16[256,132]{0,1:T(8,128)(2,1)S(1)}, bf16[256,132]{0,1:T(8,128)(2,1)S(1)}, u32[]{:S(2)}, u32[]{:S(2)}) collective-permute-start(bf16[256,132]{0,1:T(8,128)(2,1)S(1)} %collective-permute-done.7), channel_id=1, source_target_pairs={{0,30},{2,0},{4,2},{6,4},{8,6},{10,8},{12,10},{14,12},{16,14},{18,... | collective-permute-start | bytes 202760 | tf_op jit(solution)/shard_map/ppermute | solution.py:21
  52.0 8.1 %collective-permute-start.10 = (bf16[256,132]{0,1:T(8,128)(2,1)S(1)}, bf16[256,132]{0,1:T(8,128)(2,1)S(1)}, u32[]{:S(2)}, u32[]{:S(2)}) collective-permute-start(bf16[256,132]{0,1:T(8,128)(2,1)S(1)} %collective-permute-done.8), channel_id=1, source_target_pairs={{0,2},{2,4},{4,6},{6,8},{8,10},{10,12},{12,14},{14,16},{16,18},{18... | collective-permute-start | bytes 202760 | tf_op jit(solution)/shard_map/ppermute | solution.py:18
  52.0 8.1 %collective-permute-start.11 = (bf16[256,132]{0,1:T(8,128)(2,1)S(1)}, bf16[256,132]{0,1:T(8,128)(2,1)S(1)}, u32[]{:S(2)}, u32[]{:S(2)}) collective-permute-start(bf16[256,132]{0,1:T(8,128)(2,1)S(1)} %collective-permute-done.9), channel_id=1, source_target_pairs={{0,30},{2,0},{4,2},{6,4},{8,6},{10,8},{12,10},{14,12},{16,14},{18,... | collective-permute-start | bytes 202760 | tf_op jit(solution)/shard_map/ppermute | solution.py:21
  60.0 8.1 %collective-permute-start.12 = (bf16[256,132]{0,1:T(8,128)(2,1)S(1)}, bf16[256,132]{0,1:T(8,128)(2,1)S(1)}, u32[]{:S(2)}, u32[]{:S(2)}) collective-permute-start(bf16[256,132]{0,1:T(8,128)(2,1)S(1)} %collective-permute-done.10), channel_id=1, source_target_pairs={{0,2},{2,4},{4,6},{6,8},{8,10},{10,12},{12,14},{14,16},{16,18},{18... | collective-permute-start | bytes 202760 | tf_op jit(solution)/shard_map/ppermute | solution.py:18
  60.1 8.1 %collective-permute-start.13 = (bf16[256,132]{0,1:T(8,128)(2,1)S(1)}, bf16[256,132]{0,1:T(8,128)(2,1)S(1)}, u32[]{:S(2)}, u32[]{:S(2)}) collective-permute-start(bf16[256,132]{0,1:T(8,128)(2,1)S(1)} %collective-permute-done.11), channel_id=1, source_target_pairs={{0,30},{2,0},{4,2},{6,4},{8,6},{10,8},{12,10},{14,12},{16,14},{18,... | collective-permute-start | bytes 202760 | tf_op jit(solution)/shard_map/ppermute | solution.py:21
  68.2 7.9 %collective-permute-start.14 = (bf16[256,132]{0,1:T(8,128)(2,1)S(1)}, bf16[256,132]{0,1:T(8,128)(2,1)S(1)}, u32[]{:S(2)}, u32[]{:S(2)}) collective-permute-start(bf16[256,132]{0,1:T(8,128)(2,1)S(1)} %collective-permute-done.12), channel_id=1, source_target_pairs={{0,2},{2,4},{4,6},{6,8},{8,10},{10,12},{12,14},{14,16},{16,18},{18... | collective-permute-start | bytes 202760 | tf_op jit(solution)/shard_map/ppermute | solution.py:18
  88.3 3.6 %copy-start.26 = (bf16[2,68]{1,0:T(2,128)(2,1)S(1)}, bf16[2,68]{1,0:T(2,128)(2,1)}, u32[]{:S(2)}) copy-start(bf16[2,68]{1,0:T(2,128)(2,1)} %get-tuple-element.716) | copy-start | bytes 820
  132.1 2.8 %copy-start.2 = (bf16[1,128,2176]{1,2,0:T(8,128)(2,1)S(1)}, bf16[1,128,2176]{1,2,0:T(8,128)(2,1)}, u32[]{:S(2)}) copy-start(bf16[1,128,2176]{1,2,0:T(8,128)(2,1)} %copy.65) | copy-start | bytes 1671172
  137.0 75.6 %copy-start.4 = (f32[128,68]{1,0:T(8,128)S(1)}, f32[128,68]{1,0:T(8,128)}, u32[]{:S(2)}) copy-start(f32[128,68]{1,0:T(8,128)} %copy-done.3) | copy-start | bytes 104452
  210.3 4.2 %collective-permute-start.15 = (f32[256,6]{0,1:T(8,128)S(1)}, f32[256,6]{0,1:T(8,128)S(1)}, u32[]{:S(2)}, u32[]{:S(2)}) collective-permute-start(f32[256,6]{0,1:T(8,128)S(1)} %slice.28), channel_id=1, source_target_pairs={{0,1},{2,3},{4,5},{6,7},{8,9},{10,11},{12,13},{14,15},{16,17},{18,... | collective-permute-start | bytes 18440
  (20 other events, 33.1 us)
Sparse Core Ops, SparseCore 0:
  129.6 77.0 reduce-scatter.3
